TPU v7x, 256 devices: a whole 4x4x8 slice. The times are simulated.
256 devices in a mesh: seq: 64 (over z, y, core), tp: 4 (over x).
Axes of the slice: x: 4, y: 4, z: 8, core: 2. Of those that a mesh axis runs over, the one named last changes fastest.
Arguments:
- db_tokens: int32 [32768, 128], P('seq'), may hold values from 0 to 16383
- db_parent: int32 [32768, 128], P('seq'), may hold values from 0 to 126, as said below
- db_depth: int32 [32768, 128], P('seq'), may hold values from 0 to 31, as said below
- nb_rows: int32 [512, 2], P('seq'), may hold values from 0 to 32767, as said below
- seq_start: int32 [512], P('seq'), may hold values 0 or 1
- table: bfloat16 [16384, 1024], P(None, 'tp'), may hold values from -40 to 40
- depth_table: bfloat16 [32, 1024], P(None, 'tp'), may hold values from -3 to 3
- enc_gain: float32 [1024], replicated, may hold values from 0.25 to 1.75
- enc_qkv: bfloat16 [1024, 3, 1024], P('seq', None, 'tp'), may hold values from -0.1875 to 0.1875
- tree_bias: float32 [8], replicated, may hold values from 1 to 4
- enc_wo: bfloat16 [1024, 1024], P('tp', 'seq'), may hold values from -0.1875 to 0.1875
- cond_kv: bfloat16 [32768, 2, 1024], P('seq', None, 'tp'), may hold values from -150 to 150
- queries: bfloat16 [32768, 4096], P('seq', 'tp'), may hold values from -150 to 150
- cca_kv: bfloat16 [1024, 2, 512], P('seq', None, 'tp'), may hold values from -0.1875 to 0.1875
Outputs:
- attended: bfloat16 [32768, 4096], P('seq', 'tp')
Inputs may be any that keep to these rules, and one draw needn't show every extreme that they name: `db_parent`: position 0 of every stored neighbour is its own parent; every other position's parent is one of the three positions just before it. `db_depth`: position 0 has depth 0; every other position has its parent's depth plus one, capped at 31. `nb_rows`: rows 512 * i to 512 * (i + 1) - 1 of the database lie on index i of seq. Of the 16 neighbours of one index's blocks at most 1 lie on any one index; at most 32 neighbours of all blocks lie on one index, and in every draw some index holds exactly 32.
All inputs are finite; a program needn't handle non-finite values. No bound on the sum of `seq_start` on one device may be relied on, other than what follows from the above.
Results may differ from a plain program's by a relative error of at most 0.0223.
The roundings to bfloat16 on the way count: a program that leaves them out, or rounds other values in their place, can miss the bound.
Values may be sent and summed in bfloat16 or wider, within the bound.
No kernel may reach another device: no remote copies, remote signals or barrier semaphores. Data moves between devices by JAX's collectives and lax.ppermute only.
A program may use at most 128 MiB of HBM per device.

v0:
```python
import math

import jax
import jax.numpy as jnp
from jax import lax
from jax.sharding import PartitionSpec as P

HD = 128


def from_behind(value, axis, steps):
    count = lax.axis_size(axis)
    initial, last = (max(0, -steps), min(count, count - steps))
    return lax.ppermute(value, axis, [(source, source + steps) for source in range(initial, last)])


def normalize(embedded, gain):
    embedded_f = embedded.astype(jnp.float32)
    return (
        embedded_f
        * lax.rsqrt(jnp.mean(embedded_f * embedded_f, axis=-1, keepdims=True) + 1e-05)
        * gain
    ).astype(jnp.bfloat16)


def encoder_mix(normed, parents, conditioning, w_qkv, bias, head_count):
    unit_count = normed.shape[0]
    length = normed.shape[1]
    blocks = conditioning.shape[0]
    pair_count = unit_count // blocks
    cond_len = conditioning.shape[1]
    score_scale = 1.0 / math.sqrt(HD)
    projected = jnp.einsum(
        "une,eaf->unaf", normed, w_qkv, preferred_element_type=jnp.float32
    ).astype(jnp.bfloat16)
    shaped = projected.reshape(blocks, pair_count, length, 3, head_count, HD)
    query_part = shaped[:, :, :, 0]
    key_part = shaped[:, :, :, 1]
    value_part = shaped[:, :, :, 2]
    cond_keys = conditioning[:, :, 0].reshape(blocks, cond_len, head_count, HD)
    cond_values = conditioning[:, :, 1].reshape(blocks, cond_len, head_count, HD)
    self_scores = (
        jnp.einsum("cpihd,cpjhd->cphij", query_part, key_part, preferred_element_type=jnp.float32)
        * score_scale
    )
    parent_hit = (
        parents.reshape(blocks, pair_count, length)[:, :, :, None]
        == jnp.arange(length, dtype=jnp.float32)[None, None, None, :]
    ).astype(jnp.float32)
    self_scores = self_scores + bias[None, None, :, None, None] * parent_hit[:, :, None]
    cond_scores = (
        jnp.einsum("cpihd,crhd->cphir", query_part, cond_keys, preferred_element_type=jnp.float32)
        * score_scale
    )
    weights = jax.nn.softmax(jnp.concatenate([self_scores, cond_scores], axis=-1), axis=-1).astype(
        jnp.bfloat16
    )
    mixed = jnp.einsum(
        "cphij,cpjhd->cpihd", weights[..., :length], value_part, preferred_element_type=jnp.float32
    )
    mixed = mixed + jnp.einsum(
        "cphir,crhd->cpihd", weights[..., length:], cond_values, preferred_element_type=jnp.float32
    )
    return mixed.astype(jnp.bfloat16).reshape(unit_count, length, head_count * HD)


def attend(query, key_value):
    blocks, key_rows = (key_value.shape[0], key_value.shape[1])
    token_count = query.shape[1]
    head_count = query.shape[2]
    kv_heads = key_value.shape[3] // HD
    group = head_count // kv_heads
    grouped = query.reshape(blocks, token_count, kv_heads, group, HD)
    key_part = key_value[:, :, 0].reshape(blocks, key_rows, kv_heads, HD)
    value_part = key_value[:, :, 1].reshape(blocks, key_rows, kv_heads, HD)
    scores = jnp.einsum(
        "ctkgd,cpkd->ckgtp", grouped, key_part, preferred_element_type=jnp.float32
    ) * (1.0 / math.sqrt(HD))
    weights = jax.nn.softmax(scores, axis=-1).astype(jnp.bfloat16)
    output = jnp.einsum(
        "ckgtp,cpkd->ctkgd", weights, value_part, preferred_element_type=jnp.float32
    ).astype(jnp.bfloat16)
    return output.reshape(blocks, token_count, head_count, HD)


def shards(
    db_tokens,
    db_parent,
    db_depth,
    nb_rows,
    seq_start,
    table,
    depth_table,
    enc_gain,
    enc_qkv,
    tree_bias,
    enc_wo,
    cond_kv,
    queries,
    cca_kv,
):
    seq_size = lax.axis_size("seq")
    tp_size = lax.axis_size("tp")
    block_count, pair_count = nb_rows.shape
    unit_count = block_count * pair_count
    stored = db_tokens.shape[0]
    length = db_tokens.shape[1]
    slot_count = max(1, 2 * unit_count // seq_size)
    flat_rows = nb_rows.reshape(unit_count)
    holder = flat_rows // stored
    local_row = flat_rows % stored
    ordering = jnp.arange(unit_count, dtype=jnp.int32)
    earlier = jnp.sum(
        ((holder[:, None] == holder[None, :]) & (ordering[:, None] > ordering[None, :])).astype(
            jnp.int32
        ),
        axis=1,
    )
    target = holder * slot_count + earlier
    places = jnp.arange(seq_size * slot_count, dtype=jnp.int32)
    request = jnp.sum(
        jnp.where(target[None, :] == places[:, None], local_row[None, :], 0), axis=1
    ).reshape(seq_size, slot_count)
    wanted = lax.all_to_all(request, "seq", split_axis=0, concat_axis=0, tiled=True)
    tokens = jnp.take(db_tokens, wanted, axis=0)
    depths = jnp.take(db_depth, wanted, axis=0)
    parents = jnp.take(db_parent, wanted, axis=0).astype(jnp.bfloat16)
    embedded = (
        jnp.take(table, tokens, axis=0).astype(jnp.float32)
        + jnp.take(depth_table, depths, axis=0).astype(jnp.float32)
    ).astype(jnp.bfloat16)
    fetched = lax.all_to_all(embedded, "seq", split_axis=0, concat_axis=0, tiled=True)
    fetched_parents = lax.all_to_all(parents, "seq", split_axis=0, concat_axis=0, tiled=True)
    embedded = jnp.take(
        fetched.reshape((seq_size * slot_count,) + fetched.shape[2:]), target, axis=0
    )
    parents = jnp.take(
        fetched_parents.reshape(seq_size * slot_count, length), target, axis=0
    ).astype(jnp.float32)
    row_qkv, row_out = (
        lax.all_gather(enc_qkv, "seq", axis=0, tiled=True),
        lax.all_gather(enc_wo, "seq", axis=1, tiled=True),
    )
    cond_columns = cond_kv.shape[2]
    cond_len = cond_kv.shape[0] // block_count
    full_width = row_qkv.shape[0]
    head_count = row_qkv.shape[2] // HD
    conditioning = cond_kv.reshape(block_count, cond_len, 2, cond_columns)
    gathered = lax.all_gather(embedded, "tp", axis=2, tiled=True)
    normed = normalize(gathered, enc_gain)
    bias_here = lax.dynamic_slice_in_dim(tree_bias, lax.axis_index("tp") * head_count, head_count)
    mixed = encoder_mix(normed, parents, conditioning, row_qkv, bias_here, head_count).reshape(
        unit_count * length, head_count * HD
    )
    row_share = unit_count * length // tp_size
    increment = lax.psum_scatter(
        jnp.dot(mixed, row_out, preferred_element_type=jnp.float32),
        "tp",
        scatter_dimension=0,
        tiled=True,
    )
    residual = lax.dynamic_slice_in_dim(
        gathered.reshape(unit_count * length, full_width),
        lax.axis_index("tp") * row_share,
        row_share,
        0,
    )
    encoded_part = (residual.astype(jnp.float32) + increment).astype(jnp.bfloat16)
    encoded = lax.all_gather(encoded_part, "tp", axis=0, tiled=True)
    kv_weight = lax.all_gather(cca_kv, "seq", axis=0, tiled=True)
    key_rows = pair_count * length
    keys_values = jnp.einsum(
        "re,eaf->raf", encoded, kv_weight, preferred_element_type=jnp.float32
    ).astype(jnp.bfloat16)
    keys_values = keys_values.reshape(block_count, key_rows, 2, keys_values.shape[2])
    carried = from_behind(keys_values[block_count - 1], "seq", 1)
    previous = jnp.concatenate([carried[None], keys_values[: block_count - 1]], axis=0)
    head_queries = queries.shape[1] // HD
    query_heads = queries.reshape(block_count, cond_len, head_queries, HD)
    leading = attend(query_heads[:, : cond_len - 1], previous)
    trailing = attend(query_heads[:, cond_len - 1 :], keys_values)
    block_index = lax.axis_index("seq") * block_count + jnp.arange(block_count, dtype=jnp.int32)
    allowed = (block_index > 0) & (seq_start == 0)
    leading = jnp.where(allowed[:, None, None, None], leading, jnp.zeros_like(leading))
    attended = jnp.concatenate([leading, trailing], axis=1)
    return attended.reshape(block_count * cond_len, head_queries * HD)


def solution(mesh):
    in_specs = (
        P("seq", None),
        P("seq", None),
        P("seq", None),
        P("seq", None),
        P("seq"),
        P(None, "tp"),
        P(None, "tp"),
        P(),
        P("seq", None, "tp"),
        P(),
        P("tp", "seq"),
        P("seq", None, "tp"),
        P("seq", "tp"),
        P("seq", None, "tp"),
    )
    out_specs = P("seq", "tp")
    return jax.shard_map(shards, mesh=mesh, in_specs=in_specs, out_specs=out_specs, check_vma=False)
```

profile of v0, /device:TPU:32, one launch (start us, length us, event | category | flops | bytes accessed | tf_op | source)
XLA Modules:
  0.0 528.4 jit_solution(15645028171673913726)
XLA Ops:
  6.5 0.8 copy.109
  7.3 0.1 reshape.385
  7.4 0.2 convert_reduce_fusion
  7.6 0.1 select_reduce_fusion
  7.7 0.1 copy.110
  7.8 20.2 %all_to_all.22 = s32[64,1,1]{2,1,0:T(1,128)S(1)} all-to-all(s32[64,1,1]{2,1,0:T(1,128)S(1)} %copy.110), channel_id=1, replica_groups=mesh['seq'=64,'tp'=4] {'seq'}, dimensions={0} | all-to-all | bytes 512 | tf_op jit(solution)/shard_map/all_to_all | solution.py:124
  28.0 1.2 reduce.6
  29.3 0.6 gather_fusion.4
  29.9 1.5 gather_fusion.5
  31.4 0.1 bitcast_clamp_fusion.1
  31.5 0.1 and_bitcast_fusion.1
  31.6 33.1 %gather_fusion.1 = bf16[8192,256]{1,0:T(8,128)(2,1)} fusion(bf16[32,256]{1,0:T(8,128)(2,1)S(1)} %copy-done.2, s32[8192]{0:T(1024)S(1)} %get-tuple-element.16), kind=kCustom, calls=%fused_computation.4 | custom fusion | bytes 8421376 | tf_op jit(solution)/shard_map/jit(_take)/gather | solution.py:130
  64.8 35.5 %gather_fusion = bf16[8192,256]{1,0:T(8,128)(2,1)} fusion(bf16[16384,256]{1,0:T(8,128)(2,1)} %param.21, s32[8192]{0:T(1024)S(1)} %get-tuple-element.15), kind=kCustom, calls=%fused_computation.3 | custom fusion | bytes 8421376 | tf_op jit(solution)/shard_map/jit(_take)/gather | solution.py:129
  100.3 8.5 %add_convert_fusion = bf16[64,1,128,256]{3,2,1,0:T(8,128)(2,1)} fusion(bf16[64,1,128,256]{3,2,1,0:T(8,128)(2,1)} %bitcast.204, bf16[64,1,128,256]{3,2,1,0:T(8,128)(2,1)} %bitcast.205, pred[64,128]{1,0:T(8,128)(4,1)S(1)} %get-tuple-element.14, pred[64,128]{1,0:T(8,128)(4,1)S(1)} %get-tuple-element.13), kind=kLoop, calls=%fused_computation.12 | loop fusion | flops 12582912 | bytes 12599296 | tf_op jit(solution)/shard_map/convert_element_type | solution.py:131
  108.8 6.5 %all-to-all-start.1 = ((bf16[64,1,128,256]{3,2,1,0:T(8,128)(2,1)}), bf16[64,1,128,256]{3,2,1,0:T(8,128)(2,1)}, u32[]{:S(2)}, u32[]{:S(2)}) async-start(bf16[64,1,128,256]{3,2,1,0:T(8,128)(2,1)} %add_convert_fusion), calls=%async_computation.1 | async-start | bytes 8388608 | tf_op jit(solution)/shard_map/all_to_all | solution.py:132
  115.4 0.1 reshape.387
  115.5 95.1 %all-to-all-done.1 = bf16[64,1,128,256]{3,2,1,0:T(8,128)(2,1)} async-done(((bf16[64,1,128,256]{3,2,1,0:T(8,128)(2,1)}), bf16[64,1,128,256]{3,2,1,0:T(8,128)(2,1)}, u32[]{:S(2)}, u32[]{:S(2)}) %all-to-all-start.1) | async-done | bytes 4194336 | tf_op jit(solution)/shard_map/all_to_all | solution.py:132
  210.6 2.8 gather_fusion.2
  213.4 1.1 broadcast_select_fusion
  214.7 0.7 all-gather.6.cloned.1.call-update
  215.4 0.1 reduce_sum.62
  215.5 2.2 slice_reduce_fusion
  217.7 0.6 gather_fusion.6
  218.3 0.1 fusion.57
  218.3 0.6 copy.121
  219.0 6.3 %all-to-all-start.2 = ((bf16[64,1,128]{2,1,0:T(2,128)(2,1)}), bf16[64,1,128]{2,1,0:T(2,128)(2,1)S(1)}, u32[]{:S(2)}, u32[]{:S(2)}) async-start(bf16[64,1,128]{2,1,0:T(2,128)(2,1)} %copy.121), calls=%async_computation.2 | async-start | bytes 65536 | tf_op jit(solution)/shard_map/all_to_all | solution.py:133
  225.3 54.7 %all_gather.17 = bf16[256,1024]{0,1:T(8,128)(2,1)} all-gather(bf16[256,16]{0,1:T(8,128)(2,1)S(1)} %copy-done.10), channel_id=1, replica_groups=mesh['seq'=64,'tp'=4] {'seq'}, dimensions={1}, use_global_device_ids=true | all-gather | bytes 532480 | tf_op jit(solution)/shard_map/all_gather | solution.py:142
  280.2 0.8 reshape_squeeze.7
  280.9 0.1 dynamic_slice.7
  281.0 0.6 gather_fusion.3
  281.6 0.1 fusion.62
  281.7 1.1 fusion.45
  282.8 3.1 fusion
  285.9 54.5 %all-gather.6.cloned.1.call-done = bf16[1024,3,256]{2,0,1:T(8,128)(2,1)} async-done(((bf16[16,3,256]{2,0,1:T(8,128)(2,1)}), bf16[1024,3,256]{2,0,1:T(8,128)(2,1)}) %all-gather.6.cloned.1.call-update) | async-done | bytes 1572880 | tf_op jit(solution)/shard_map/all_gather | solution.py:141
  340.4 7.9 %fusion.16 = bf16[16,128,3,256]{3,1,2,0:T(8,128)(2,1)} fusion(bf16[16,128,1024]{2,1,0:T(8,128)(2,1)} %all-gather.4.cloned.1.call-done, f32[1024]{0:T(1024)S(1)} %copy-done.12, f32[16,128]{1,0:T(8,128)S(1)} %add_rsqrt_fusion, bf16[1024,3,256]{2,0,1:T(8,128)(2,1)} %all-gather.6.cloned.1.call-done), kind=kOutput, calls=%fused_computation.28 | convolution fusion | flops 3231186944 | bytes 8925184 | tf_op jit(solution)/shard_map/une,eaf->unaf/dot_general | solution.py:33
  348.3 3.8 reshape.389
  352.0 3.2 fusion.69
  355.2 0.5 fusion.71
  355.7 0.9 fusion.70
  356.6 0.6 fusion.19
  357.2 0.6 divide_convert_fusion.1
  357.8 1.9 copy.150
  359.8 1.7 fusion.40
  361.5 0.5 fusion.22
  362.0 0.8 copy.130
  362.8 4.5 fusion.37
  367.4 82.4 %reduce-scatter.2.cloned.1.call-done = f32[512,1024]{1,0:T(8,128)} async-done(((f32[2048,1024]{1,0:T(8,128)}), f32[512,1024]{1,0:T(8,128)}) %reduce-scatter.2.cloned.1.call-update) | async-done | bytes 2097168 | tf_op jit(solution)/shard_map/reduce_scatter | solution.py:156
  449.8 3.2 add_convert_fusion.1
  453.1 0.3 copy.157
  453.3 0.1 slice.90
  453.4 44.4 %all_gather.19 = bf16[1024,2,128]{2,0,1:T(8,128)(2,1)S(1)} all-gather(bf16[16,2,128]{2,0,1:T(8,128)(2,1)S(1)} %copy.131), channel_id=1, replica_groups=mesh['seq'=64,'tp'=4] {'seq'}, dimensions={0}, use_global_device_ids=true | all-gather | bytes 532480 | tf_op jit(solution)/shard_map/all_gather | solution.py:170
  497.8 5.9 %all-gather.8.cloned.1.call-done = bf16[2048,1024]{1,0:T(8,128)(2,1)} async-done(((bf16[512,1024]{1,0:T(8,128)(2,1)}), bf16[2048,1024]{1,0:T(8,128)(2,1)}) %all-gather.8.cloned.1.call-update) | async-done | bytes 4194320 | tf_op jit(solution)/shard_map/all_gather | solution.py:169
  503.7 3.4 fusion.13
  507.2 1.9 collective-permute-start
  509.2 0.3 fusion.72
  509.5 0.2 fusion.55
  509.7 0.2 fusion.33
  509.9 5.7 %collective-permute-done = bf16[256,2,128]{2,0,1:T(8,128)(2,1)S(1)} collective-permute-done((bf16[256,2,128]{2,0,1:T(8,128)(2,1)S(1)}, bf16[256,2,128]{2,0,1:T(8,128)(2,1)S(1)}, u32[]{:S(2)}, u32[]{:S(2)}) %collective-permute-start) | collective-permute-done | bytes 131104 | tf_op jit(solution)/shard_map/ppermute | solution.py:14
  515.6 0.8 bitcast_reduce_fusion
  516.4 1.4 fusion.11
  517.9 1.9 fusion.34
  519.8 0.2 pad_maximum_fusion
  520.0 0.7 copy.135
  520.7 1.2 copy.186
  (56 shorter events, 0.6 us)
Async XLA Ops:
  6.5 22.7 %copy-start = (s32[512,128]{1,0:T(8,128)S(1)}, s32[512,128]{1,0:T(8,128)}, u32[]{:S(2)}) copy-start(s32[512,128]{1,0:T(8,128)} %param.16) | copy-start | bytes 786436
  6.5 25.1 %copy-start.2 = (bf16[32,256]{1,0:T(8,128)(2,1)S(1)}, bf16[32,256]{1,0:T(8,128)(2,1)}, u32[]{:S(2)}) copy-start(bf16[32,256]{1,0:T(8,128)(2,1)} %param.22) | copy-start | bytes 49156
  108.8 101.8 %all-to-all-start.1 = ((bf16[64,1,128,256]{3,2,1,0:T(8,128)(2,1)}), bf16[64,1,128,256]{3,2,1,0:T(8,128)(2,1)}, u32[]{:S(2)}, u32[]{:S(2)}) async-start(bf16[64,1,128,256]{3,2,1,0:T(8,128)(2,1)} %add_convert_fusion), calls=%async_computation.1 | async-start | bytes 8388608 | tf_op jit(solution)/shard_map/all_to_all | solution.py:132
  115.3 100.1 %copy-start.6 = (bf16[512,2,256]{2,1,0:T(2,128)(2,1)S(1)}, bf16[512,2,256]{2,1,0:T(2,128)(2,1)}, u32[]{:S(2)}) copy-start(bf16[512,2,256]{2,1,0:T(2,128)(2,1)} %param.27) | copy-start | bytes 1572868
  115.3 102.3 %copy-start.9 = (s32[512,128]{1,0:T(8,128)S(1)}, s32[512,128]{1,0:T(8,128)}, u32[]{:S(2)}) copy-start(s32[512,128]{1,0:T(8,128)} %param.17) | copy-start | bytes 786436
  115.3 110.0 %copy-start.10 = (bf16[256,16]{0,1:T(8,128)(2,1)S(1)}, bf16[256,16]{0,1:T(8,128)(2,1)}, u32[]{:S(2)}) copy-start(bf16[256,16]{0,1:T(8,128)(2,1)} %param.26) | copy-start | bytes 24580
  115.4 167.5 %all-gather.4.cloned.1.call-start = ((), (), s32[]{:S(2)}) async-start(), calls=%async_computation.4 | async-start | bytes 5242880 | tf_op jit(solution)/shard_map/all_gather | solution.py:149
  210.6 70.3 %copy-start.13 = (f32[8]{0:T(128)S(1)}, f32[8]{0:T(128)}, u32[]{:S(2)}) copy-start(f32[8]{0:T(128)} %param.25) | copy-start | bytes 100
  214.6 125.8 %all-gather.6.cloned.1.call-start = ((), (), s32[]{:S(2)}) async-start(), calls=%async_computation.5 | async-start | bytes 1597440 | tf_op jit(solution)/shard_map/all_gather | solution.py:141
  215.5 124.9 %copy-start.12 = (f32[1024]{0:T(1024)S(1)}, f32[1024]{0:T(1024)}, u32[]{:S(2)}) copy-start(f32[1024]{0:T(1024)} %param.23) | copy-start | bytes 12292
  219.0 62.0 %all-to-all-start.2 = ((bf16[64,1,128]{2,1,0:T(2,128)(2,1)}), bf16[64,1,128]{2,1,0:T(2,128)(2,1)S(1)}, u32[]{:S(2)}, u32[]{:S(2)}) async-start(bf16[64,1,128]{2,1,0:T(2,128)(2,1)} %copy.121), calls=%async_computation.2 | async-start | bytes 65536 | tf_op jit(solution)/shard_map/all_to_all | solution.py:133
  225.3 224.5 %reduce-scatter.2.cloned.1.call-start = ((), (), s32[]{:S(2)}) async-start(), calls=%async_computation.6 | async-start | bytes 10485760 | tf_op jit(solution)/shard_map/reduce_scatter | solution.py:156
  352.0 3.7 copy-start.3
  356.6 1.2 copy-start.4
  357.8 3.7 copy-start.8
  359.8 3.0 copy-start.5
  367.3 85.7 %copy-start.11 = (bf16[16,2,128]{2,1,0:T(2,128)(2,1)S(1)}, bf16[16,2,128]{2,1,0:T(2,128)(2,1)}, u32[]{:S(2)}) copy-start(bf16[16,2,128]{2,1,0:T(2,128)(2,1)} %param.29) | copy-start | bytes 24580
  367.4 85.7 %copy-start.7 = (bf16[512,1024]{1,0:T(8,128)(2,1)S(1)}, bf16[512,1024]{1,0:T(8,128)(2,1)}, u32[]{:S(2)}) copy-start(bf16[512,1024]{1,0:T(8,128)(2,1)} %param.28) | copy-start | bytes 3145732
  367.4 136.3 %all-gather.8.cloned.1.call-start = ((), (), s32[]{:S(2)}) async-start(), calls=%async_computation.7 | async-start | bytes 5242880 | tf_op jit(solution)/shard_map/all_gather | solution.py:169
  449.8 48.0 %copy-start.14 = (s32[8]{0:T(128)S(1)}, s32[8]{0:T(128)}, u32[]{:S(2)}) copy-start(s32[8]{0:T(128)} %param.20) | copy-start | bytes 100
  507.2 8.4 %collective-permute-start = (bf16[256,2,128]{2,0,1:T(8,128)(2,1)S(1)}, bf16[256,2,128]{2,0,1:T(8,128)(2,1)S(1)}, u32[]{:S(2)}, u32[]{:S(2)}) collective-permute-start(bf16[256,2,128]{2,0,1:T(8,128)(2,1)S(1)} %slice.86), channel_id=1, source_target_pairs={{0,4},{4,8},{8,12},{12,16},{16,20},{20,24},{24,28},{28,32},{32,36}... | collective-permute-start | bytes 393224 | tf_op jit(solution)/shard_map/ppermute | solution.py:14
  517.9 4.0 copy-start.1
Sparse Core Ops, SparseCore 0:
  214.7 51.0 all-gather.3
  268.4 71.8 all-gather.5
  367.5 82.3 reduce-scatter.1
  453.1 50.5 all-gather.7
where the time goes:
time: 529 us; the launch traced here: 528 us
  waiting for transfers between devices  244 us (46%)
  blocking collectives  119 us (22%)
  local copies, waits for them, and re-layouts  91.8 us (17%)
  matrix products  22.6 us (4%)
  other arithmetic  21.9 us (4%)
  starting transfers between devices  14.9 us (3%)
  between operations  13.6 us (3%)
    all_to_all x1, waiting for transfers between devices, shards(): lax.all_to_all(embedded, 'seq', split_axis=0, concat_axis=0, tiled=True)  95.1 us
    reduce_scatter x1, waiting for transfers between devices, shards(): lax.psum_scatter(jnp.dot(mixed, row_out, preferred_element_type=jnp.float...  82.4 us
    all_gather x1, blocking collectives, shards(): lax.all_gather(enc_wo, 'seq', axis=1, tiled=True)  54.7 us
    all_gather x1, waiting for transfers between devices, shards(): lax.all_gather(enc_qkv, 'seq', axis=0, tiled=True)  54.5 us
    all_gather x1, blocking collectives, shards(): kv_weight = lax.all_gather(cca_kv, 'seq', axis=0, tiled=True)  44.4 us
    gather x1, local copies, waits for them, and re-layouts, shards(): jnp.take(table, tokens, axis=0).astype(jnp.float32)  35.5 us
    gather x1, local copies, waits for them, and re-layouts, shards(): jnp.take(depth_table, depths, axis=0).astype(jnp.float32)  33.1 us
    all_to_all x1, blocking collectives, shards(): lax.all_to_all(request, 'seq', split_axis=0, concat_axis=0, tiled=True)  20.2 us
  transfers between devices with their start and end apart: 7, of which 5 were waited for; matrix products, arithmetic and copies ran while one was open for 2% of the time, Pallas kernels for 0%

commit v1 on v0

v1 whole, which is shorter than its diff:
```python
import math

import jax
import jax.numpy as jnp
from jax import lax
from jax.sharding import PartitionSpec as P

HD = 128
SCALE = 1.0 / math.sqrt(HD)


def exchange(value, axis):
    return lax.all_to_all(value, axis, split_axis=0, concat_axis=0, tiled=True)


def normalize(embedded, gain):
    embedded_f = embedded.astype(jnp.float32)
    return (
        embedded_f
        * lax.rsqrt(jnp.mean(embedded_f * embedded_f, axis=-1, keepdims=True) + 1e-05)
        * gain
    ).astype(jnp.bfloat16)


def encoder_mix(normed, parents, cond_keys, cond_values, w_qkv, bias):
    unit_count, length, _ = normed.shape
    blocks, cond_len, head_count, _ = cond_keys.shape
    pair_count = unit_count // blocks
    projected = jnp.einsum(
        "une,eaf->unaf", normed, w_qkv, preferred_element_type=jnp.float32
    ).astype(jnp.bfloat16)
    shaped = projected.reshape(blocks, pair_count, length, 3, head_count, HD)
    query_part = shaped[:, :, :, 0]
    key_part = shaped[:, :, :, 1]
    value_part = shaped[:, :, :, 2]
    self_scores = (
        jnp.einsum("cpihd,cpjhd->cphij", query_part, key_part, preferred_element_type=jnp.float32)
        * SCALE
    )
    parent_hit = (
        parents.reshape(blocks, pair_count, length)[:, :, :, None]
        == jnp.arange(length, dtype=parents.dtype)[None, None, None, :]
    ).astype(jnp.float32)
    self_scores = self_scores + bias[None, None, :, None, None] * parent_hit[:, :, None]
    cond_scores = (
        jnp.einsum("cpihd,crhd->cphir", query_part, cond_keys, preferred_element_type=jnp.float32)
        * SCALE
    )
    weights = jax.nn.softmax(jnp.concatenate([self_scores, cond_scores], axis=-1), axis=-1).astype(
        jnp.bfloat16
    )
    mixed = jnp.einsum(
        "cphij,cpjhd->cpihd", weights[..., :length], value_part, preferred_element_type=jnp.float32
    )
    mixed = mixed + jnp.einsum(
        "cphir,crhd->cpihd", weights[..., length:], cond_values, preferred_element_type=jnp.float32
    )
    return mixed.astype(jnp.bfloat16).reshape(unit_count, length, head_count * HD)


def attend(query, key_value):
    blocks, key_rows = (key_value.shape[0], key_value.shape[1])
    token_count = query.shape[1]
    head_count = query.shape[2]
    kv_heads = key_value.shape[3] // HD
    group = head_count // kv_heads
    grouped = query.reshape(blocks, token_count, kv_heads, group, HD)
    key_part = key_value[:, :, 0].reshape(blocks, key_rows, kv_heads, HD)
    value_part = key_value[:, :, 1].reshape(blocks, key_rows, kv_heads, HD)
    scores = (
        jnp.einsum("ctkgd,cpkd->ckgtp", grouped, key_part, preferred_element_type=jnp.float32)
        * SCALE
    )
    weights = jax.nn.softmax(scores, axis=-1).astype(jnp.bfloat16)
    output = jnp.einsum(
        "ckgtp,cpkd->ctkgd", weights, value_part, preferred_element_type=jnp.float32
    ).astype(jnp.bfloat16)
    return output.reshape(blocks, token_count, head_count, HD)


def shards(
    db_tokens,
    db_parent,
    db_depth,
    nb_rows,
    seq_start,
    table,
    depth_table,
    enc_gain,
    enc_qkv,
    tree_bias,
    enc_wo,
    cond_kv,
    queries,
    cca_kv,
):
    seq_size = lax.axis_size("seq")
    tp_size = lax.axis_size("tp")
    block_count, pair_count = nb_rows.shape
    unit_count = block_count * pair_count
    stored, length = db_tokens.shape
    columns = table.shape[1]
    width = columns * tp_size
    rows_here = enc_qkv.shape[0]

    share = jnp.concatenate(
        [
            enc_qkv.transpose(1, 0, 2).reshape(3 * rows_here, columns),
            enc_wo.T,
            cca_kv.reshape(rows_here, columns),
        ],
        axis=0,
    )
    shares = lax.all_gather(share, ("seq", "tp"), axis=0).reshape(
        seq_size, tp_size, 5, rows_here, columns
    )
    w_qkv = (
        shares[:, :, :3].transpose(0, 3, 2, 1, 4).reshape(width, 3, width)
    )
    w_out = shares[:, :, 3].transpose(0, 2, 1, 3).reshape(width, width)
    kv_cols = cca_kv.shape[2]
    w_cca = (
        shares[:, :, 4]
        .reshape(seq_size, tp_size, rows_here, 2, kv_cols)
        .transpose(0, 2, 3, 1, 4)
        .reshape(width, 2, tp_size * kv_cols)
    )

    cond_len = cond_kv.shape[0] // block_count
    my_blocks = block_count // tp_size
    cond = exchange(
        cond_kv.reshape(tp_size, my_blocks * cond_len, 2 * columns), "tp"
    ).reshape(tp_size, my_blocks, cond_len, 2, columns // HD, HD)
    cond = cond.transpose(3, 1, 2, 0, 4, 5).reshape(2, my_blocks, cond_len, width // HD, HD)

    flat_rows = nb_rows.reshape(unit_count)
    holder = flat_rows // stored
    local_row = flat_rows % stored
    places = jnp.arange(seq_size, dtype=jnp.int32)
    request = jnp.sum(
        jnp.where(holder[None, :] == places[:, None], local_row[None, :], 0), axis=1
    )
    request = jnp.broadcast_to(request[:, None], (seq_size, 16))
    wanted = exchange(request, "seq")[:, 0]
    reply = jnp.concatenate(
        [
            jnp.take(db_tokens, wanted, axis=0),
            jnp.take(db_depth, wanted, axis=0),
            jnp.take(db_parent, wanted, axis=0),
        ],
        axis=1,
    )
    fetched = jnp.take(exchange(reply, "seq"), holder, axis=0)
    tokens = fetched[:, :length].reshape(unit_count * length)
    depths = fetched[:, length : 2 * length].reshape(unit_count * length)
    parents = fetched[:, 2 * length :]
    depth_hit = (
        depths[:, None] == jnp.arange(depth_table.shape[0], dtype=jnp.int32)[None, :]
    ).astype(jnp.bfloat16)
    embedded = (
        jnp.take(table, tokens, axis=0).astype(jnp.float32)
        + jnp.dot(depth_hit, depth_table, preferred_element_type=jnp.float32)
    ).astype(jnp.bfloat16)

    my_units = unit_count // tp_size
    pieces = exchange(embedded.reshape(tp_size, my_units * length, columns), "tp")
    embedded = pieces.transpose(1, 0, 2).reshape(my_units, length, width)
    parents = lax.dynamic_slice_in_dim(parents, lax.axis_index("tp") * my_units, my_units)
    normed = normalize(embedded, enc_gain)
    mixed = encoder_mix(normed, parents, cond[0], cond[1], w_qkv, tree_bias)
    increment = jnp.einsum("unf,ef->une", mixed, w_out, preferred_element_type=jnp.float32)
    encoded = (embedded.astype(jnp.float32) + increment).astype(jnp.bfloat16)
    keys_values = jnp.einsum(
        "une,eaf->unaf", encoded, w_cca, preferred_element_type=jnp.float32
    ).astype(jnp.bfloat16)
    outgoing = keys_values.reshape(my_units * length, 2, tp_size, kv_cols).transpose(2, 0, 1, 3)
    key_rows = pair_count * length
    keys_values = exchange(
        outgoing.reshape(tp_size, my_units * length, 2 * kv_cols), "tp"
    ).reshape(block_count, key_rows, 2, kv_cols)
    carried = lax.ppermute(
        keys_values[block_count - 1], "seq", [(s, s + 1) for s in range(seq_size - 1)]
    )
    previous = jnp.concatenate([carried[None], keys_values[: block_count - 1]], axis=0)
    head_queries = queries.shape[1] // HD
    query_heads = queries.reshape(block_count, cond_len, head_queries, HD)
    leading = attend(query_heads[:, : cond_len - 1], previous)
    trailing = attend(query_heads[:, cond_len - 1 :], keys_values)
    block_index = lax.axis_index("seq") * block_count + jnp.arange(block_count, dtype=jnp.int32)
    allowed = (block_index > 0) & (seq_start == 0)
    leading = jnp.where(allowed[:, None, None, None], leading, jnp.zeros_like(leading))
    attended = jnp.concatenate([leading, trailing], axis=1)
    return attended.reshape(block_count * cond_len, head_queries * HD)


def solution(mesh):
    in_specs = (
        P("seq", None),
        P("seq", None),
        P("seq", None),
        P("seq", None),
        P("seq"),
        P(None, "tp"),
        P(None, "tp"),
        P(),
        P("seq", None, "tp"),
        P(),
        P("tp", "seq"),
        P("seq", None, "tp"),
        P("seq", "tp"),
        P("seq", None, "tp"),
    )
    out_specs = P("seq", "tp")
    return jax.shard_map(shards, mesh=mesh, in_specs=in_specs, out_specs=out_specs, check_vma=False)
```

time: 529 us -> 250 us (0.47)
  waiting for transfers between devices: 244 us -> 86.7 us
  blocking collectives: 119 us -> 0 us
  starting transfers between devices: 14.9 us -> 32.8 us
  other arithmetic: 21.9 us -> 7.25 us
  local copies, waits for them, and re-layouts: 91.8 us -> 84.7 us
    all_gather x2 -> x0, blocking collectives: 99.1 us -> none  [the longest x1 54.7 us: shards(): lax.all_gather(enc_wo, 'seq', axis=1, tiled=True)]
    reduce_scatter x1 -> x0, waiting for transfers between devices: 82.4 us -> none  [shards(): lax.psum_scatter(jnp.dot(mixed, row_out, preferred_element_type=jnp.float...]
    all_to_all x2 -> x5, waiting for transfers between devices: 95.1 us -> 44.2 us  [exchange(): return lax.all_to_all(value, axis, split_axis=0, concat_axis=0, tiled=True)]
    gather x6 -> x4, local copies, waits for them, and re-layouts: 39.3 us -> 4.27 us  [the longest x1 1.55 us: shards(): jnp.take(db_depth, wanted, axis=0)]
    transpose x0 -> x5, local copies, waits for them, and re-layouts: none -> 27 us  [the longest x2 18 us: shards(): w_qkv = shares[:, :, :3].transpose(0, 3, 2, 1, 4).reshape(width, 3, width)]
    gather x1, local copies, waits for them, and re-layouts: 35.5 us -> 11.1 us  [shards(): jnp.take(table, tokens, axis=0).astype(jnp.float32)]
    all_gather x3 -> x1, waiting for transfers between devices: 60.4 us -> 36.6 us  [shards(): lax.all_gather(share, ('seq', 'tp'), axis=0)]
    all_to_all x1 -> x0, blocking collectives: 20.2 us -> none  [shards(): lax.all_to_all(request, 'seq', split_axis=0, concat_axis=0, tiled=True)]
  transfers between devices with their start and end apart: 7 -> 7, of which waited for: 5 -> 6; matrix products, arithmetic and copies ran while one was open for 2% -> 12% of each run, Pallas kernels for 0% -> 0%
where the time goes in v1:
time: 250 us; the launch traced here: 249 us
  waiting for transfers between devices  86.7 us (35%)
  local copies, waits for them, and re-layouts  84.7 us (34%)
  starting transfers between devices  32.8 us (13%)
  matrix products  23.9 us (10%)
  between operations  13.9 us (6%)
  other arithmetic  7.25 us (3%)
    all_to_all x5, waiting for transfers between devices, exchange(): return lax.all_to_all(value, axis, split_axis=0, concat_axis=0, tiled=True)  44.2 us
    all_gather x1, waiting for transfers between devices, shards(): lax.all_gather(share, ('seq', 'tp'), axis=0)  36.6 us
    all_to_all x5, starting transfers between devices, exchange(): return lax.all_to_all(value, axis, split_axis=0, concat_axis=0, tiled=True)  30.9 us
    transpose x2, local copies, waits for them, and re-layouts, shards(): w_qkv = shares[:, :, :3].transpose(0, 3, 2, 1, 4).reshape(width, 3, width)  18 us
    gather x1, local copies, waits for them, and re-layouts, shards(): jnp.take(table, tokens, axis=0).astype(jnp.float32)  11.1 us
    reshape x1, local copies, waits for them, and re-layouts, shards(): w_qkv = shares[:, :, :3].transpose(0, 3, 2, 1, 4).reshape(width, 3, width)  11 us
    transpose x2, local copies, waits for them, and re-layouts, shards(): w_out = shares[:, :, 3].transpose(0, 2, 1, 3).reshape(width, width)  7.57 us
    dot_general x1, matrix products, encoder_mix(): jnp.einsum('une,eaf->unaf', normed, w_qkv, preferred_element_type=jnp.flo...  6.4 us
  transfers between devices with their start and end apart: 7, of which 6 were waited for; matrix products, arithmetic and copies ran while one was open for 12% of the time, Pallas kernels for 0%

profile of v1, /device:TPU:32, one launch (start us, length us, event | category | flops | bytes accessed | tf_op | source)
XLA Modules:
  0.0 249.3 jit_solution(1685811043052644031)
XLA Ops:
  6.5 0.8 copy.215
  7.3 1.4 pad_maximum_fusion.2
  8.7 0.8 copy.135
  9.7 0.8 broadcast_in_dim.81
  10.4 11.8 %all-to-all-start = ((s32[64,1,16]{2,1,0:T(1,128)}), s32[64,1,16]{2,1,0:T(1,128)S(1)}, u32[]{:S(2)}, u32[]{:S(2)}) async-start(s32[64,1,16]{2,1,0:T(1,128)} %broadcast_in_dim.81), calls=%async_computation | async-start | bytes 65536 | tf_op jit(solution)/shard_map/all_to_all | solution.py:13
  22.3 8.5 %all-to-all-done = s32[64,1,16]{2,1,0:T(1,128)S(1)} async-done(((s32[64,1,16]{2,1,0:T(1,128)}), s32[64,1,16]{2,1,0:T(1,128)S(1)}, u32[]{:S(2)}, u32[]{:S(2)}) %all-to-all-start) | async-done | bytes 4128 | tf_op jit(solution)/shard_map/all_to_all | solution.py:13
  30.9 0.6 gather_fusion.2
  31.5 1.5 gather_fusion.3
  33.1 1.5 gather_fusion.4
  34.7 0.7 copy.136
  35.4 5.5 %all-to-all-start.1 = ((s32[64,1,384]{2,1,0:T(1,128)}), s32[64,1,384]{2,1,0:T(1,128)S(1)}, u32[]{:S(2)}, u32[]{:S(2)}) async-start(s32[64,1,384]{2,1,0:T(1,128)} %copy.136), calls=%async_computation.1 | async-start | bytes 196608 | tf_op jit(solution)/shard_map/all_to_all | solution.py:13
  41.0 1.1 reshape.350
  42.2 8.4 %all-to-all-done.1 = s32[64,1,384]{2,1,0:T(1,128)S(1)} async-done(((s32[64,1,384]{2,1,0:T(1,128)}), s32[64,1,384]{2,1,0:T(1,128)S(1)}, u32[]{:S(2)}, u32[]{:S(2)}) %all-to-all-start.1) | async-done | bytes 98336 | tf_op jit(solution)/shard_map/all_to_all | solution.py:13
  50.6 4.6 %all-to-all-start.3 = ((bf16[4,128,512]{2,1,0:T(8,128)(2,1)}), bf16[4,128,512]{2,1,0:T(8,128)(2,1)S(1)}, u32[]{:S(2)}, u32[]{:S(2)}) async-start(bf16[4,128,512]{2,1,0:T(8,128)(2,1)} %reshape.350), calls=%async_computation.3 | async-start | bytes 1048576 | tf_op jit(solution)/shard_map/all_to_all | solution.py:13
  55.1 0.6 gather_fusion
  55.8 11.1 %gather_fusion.1 = bf16[2048,256]{1,0:T(8,128)(2,1)S(1)} fusion(bf16[16384,256]{1,0:T(8,128)(2,1)} %param.21, s32[2048]{0:T(1024)S(1)} %broadcast_clamp_fusion), kind=kCustom, calls=%fused_computation.4 | custom fusion | bytes 2105344 | tf_op jit(solution)/shard_map/jit(_take)/gather | solution.py:161
  67.0 2.8 %fusion.3 = bf16[2048,256]{1,0:T(8,128)(2,1)} fusion(bf16[32,256]{1,0:T(8,128)(2,1)S(1)} %copy-done.10, bf16[2048,256]{1,0:T(8,128)(2,1)S(1)} %gather_fusion.1, pred[2048]{0:T(1024)(128)(4,1)S(1)} %compare_and_fusion, s32[2048]{0:T(1024)S(1)} %get-tuple-element.18), kind=kOutput, calls=%fused_computation.18 | convolution fusion | flops 35717120 | bytes 2123776 | tf_op jit(solution)/shard_map/dot_general | solution.py:162
  69.8 4.8 %all-to-all-start.2 = ((bf16[4,512,256]{2,1,0:T(8,128)(2,1)}), bf16[4,512,256]{2,1,0:T(8,128)(2,1)S(1)}, u32[]{:S(2)}, u32[]{:S(2)}) async-start(bf16[4,512,256]{2,1,0:T(8,128)(2,1)} %bitcast.7), calls=%async_computation.2 | async-start | bytes 2097152 | tf_op jit(solution)/shard_map/all_to_all | solution.py:13
  74.6 0.7 fusion.40
  75.5 0.5 fusion.50
  76.0 0.8 copy.148
  76.8 13.2 %all-to-all-done.2 = bf16[4,512,256]{2,1,0:T(8,128)(2,1)S(1)} async-done(((bf16[4,512,256]{2,1,0:T(8,128)(2,1)}), bf16[4,512,256]{2,1,0:T(8,128)(2,1)S(1)}, u32[]{:S(2)}, u32[]{:S(2)}) %all-to-all-start.2) | async-done | bytes 1048608 | tf_op jit(solution)/shard_map/all_to_all | solution.py:13
  90.2 1.4 copy.138
  91.5 2.1 reshape.369
  93.9 0.3 fusion.25
  94.3 0.8 copy.139
  95.1 0.8 reshape.421
  95.9 36.6 %all-gather.3.cloned.1.call-done = bf16[20480,256]{1,0:T(8,128)(2,1)} async-done(((bf16[80,256]{1,0:T(8,128)(2,1)}), bf16[20480,256]{1,0:T(8,128)(2,1)}) %all-gather.3.cloned.1.call-update) | async-done | bytes 10485776 | tf_op jit(solution)/shard_map/all_gather | solution.py:114
  132.4 4.9 %slice_bitcast_fusion.1 = (bf16[64,16,4,256]{3,1,2,0:T(8,128)(2,1)}, bf16[64,4,1,16,256]{4,3,2,1,0:T(8,128)(2,1)}) fusion(bf16[64,4,5,16,256]{4,3,2,1,0:T(8,128)(2,1)} %bitcast.201), kind=kLoop, calls=%fused_computation.24 | loop fusion | bytes 8388608 | tf_op jit(solution)/shard_map/transpose | solution.py:120
  137.3 6.2 %slice_bitcast_fusion = bf16[64,16,3,4,256]{4,1,2,3,0:T(8,128)(2,1)} fusion(bf16[64,4,5,16,256]{4,3,2,1,0:T(8,128)(2,1)} %bitcast.202), kind=kLoop, calls=%fused_computation.5 | loop fusion | bytes 12582912 | tf_op jit(solution)/shard_map/transpose | solution.py:118
  143.5 2.5 %reshape_squeeze.3 = bf16[64,4,16,2,128]{4,3,2,1,0:T(2,128)(2,1)S(1)} reshape(bf16[64,4,1,16,256]{4,3,2,1,0:T(8,128)(2,1)} %get-tuple-element.9) | data formatting | bytes 4194304 | tf_op jit(solution)/shard_map/reshape;squeeze | solution.py:124
  146.0 2.5 copy.211
  148.5 4.1 %reshape.427 = bf16[1024,2,512,1]{2,0,1,3:T(8,128)(2,1)} reshape(bf16[64,16,2,4,128]{4,3,1,0,2:T(4,128)(2,1)} %bitcast.203) | data formatting | bytes 4194304 | tf_op jit(solution)/shard_map/reshape | solution.py:126
  152.6 11.8 %copy.140 = bf16[64,16,3,4,256]{4,3,1,0,2:T(4,128)(2,1)} copy(bf16[64,16,3,4,256]{4,1,2,3,0:T(8,128)(2,1)} %slice_bitcast_fusion) | data formatting | bytes 12582912 | tf_op jit(solution)/shard_map/transpose | solution.py:118
  164.4 11.0 %reshape.422 = bf16[1024,3,1024,1]{2,0,1,3:T(8,128)(2,1)} reshape(bf16[64,16,3,4,256]{4,3,1,0,2:T(4,128)(2,1)} %copy.140) | data formatting | bytes 12582912 | tf_op jit(solution)/shard_map/reshape | solution.py:118
  175.5 6.4 %convolution_convert_fusion = bf16[4,128,3,1024]{3,1,2,0:T(8,128)(2,1)S(1)} fusion(bf16[1024,3,1024,1]{2,0,1,3:T(8,128)(2,1)} %reshape.422, bf16[4,128,1024,1]{2,1,0,3:T(8,128)(2,1)S(1)} %reshape.421), kind=kOutput, calls=%fused_computation.19 | convolution fusion | flops 3222798336 | bytes 10485760 | tf_op jit(solution)/shard_map/une,eaf->unaf/dot_general | solution.py:29
  181.9 0.8 copy.182
  182.9 0.5 fusion.53
  183.4 0.4 copy-done.8
  183.9 0.9 fusion.52
  184.8 0.5 fusion.4
  185.3 1.7 divide_convert_fusion.1
  187.0 0.8 copy.173
  187.8 2.7 %copy.149 = bf16[64,16,4,256]{3,2,1,0:T(4,128)(2,1)S(1)} copy(bf16[64,16,4,256]{3,1,2,0:T(8,128)(2,1)} %get-tuple-element.8) | data formatting | bytes 4194304 | tf_op jit(solution)/shard_map/transpose | solution.py:120
  190.5 2.7 %reshape.425 = bf16[1024,1024,1]{1,0,2:T(8,128)(2,1)} reshape(bf16[64,16,4,256]{3,2,1,0:T(4,128)(2,1)S(1)} %copy.149) | data formatting | bytes 4194304 | tf_op jit(solution)/shard_map/reshape | solution.py:120
  193.2 1.7 fusion.26
  194.9 2.7 %fusion.10 = bf16[2,2,128,8,128]{2,4,3,1,0:T(8,128)(2,1)} fusion(f32[2,2,8,128,128]{4,3,2,1,0:T(8,128)S(1)} %fusion.26, bf16[2,64,8,128,1]{3,1,2,4,0:T(8,128)(2,1)S(1)} %bitcast.213, bf16[2,2,8,128,192]{3,4,2,1,0:T(8,128)(2,1)} %divide_convert_fusion.1), kind=kOutput, calls=%fused_computation.28 | convolution fusion | flops 68157440 | bytes 3932160 | tf_op jit(solution)/shard_map/cphir,crhd->cpihd/dot_general | solution.py:55
  197.6 4.9 %convolution_convert_fusion.1 = bf16[4,128,2,512]{3,1,2,0:T(8,128)(2,1)S(1)} fusion(bf16[1024,2,512,1]{2,0,1,3:T(8,128)(2,1)} %reshape.427, f32[4,128,1024]{2,1,0:T(8,128)S(1)} %copy-done.4, bf16[4,128,1024]{1,2,0:T(8,128)(2,1)} %bitcast.212, bf16[1024,1024,1]{1,0,2:T(8,128)(2,1)} %reshape.425), kind=kOutput, calls=%fused_computation.34 | convolution fusion | flops 2149056512 | bytes 8388608 | tf_op jit(solution)/shard_map/une,eaf->unaf/dot_general | solution.py:173
  202.6 0.3 reshape.355
  202.9 1.5 copy.153
  204.4 4.3 %all-to-all-start.4 = ((bf16[4,512,256]{1,2,0:T(8,128)(2,1)}), bf16[4,512,256]{1,2,0:T(8,128)(2,1)S(1)}, u32[]{:S(2)}, u32[]{:S(2)}) async-start(bf16[4,512,256]{1,2,0:T(8,128)(2,1)} %bitcast.37), calls=%async_computation.4 | async-start | bytes 2097152 | tf_op jit(solution)/shard_map/all_to_all | solution.py:13
  208.9 1.0 copy-done.3
  210.0 14.1 %all-to-all-done.4 = bf16[4,512,256]{1,2,0:T(8,128)(2,1)S(1)} async-done(((bf16[4,512,256]{1,2,0:T(8,128)(2,1)}), bf16[4,512,256]{1,2,0:T(8,128)(2,1)S(1)}, u32[]{:S(2)}, u32[]{:S(2)}) %all-to-all-start.4) | async-done | bytes 1048608 | tf_op jit(solution)/shard_map/all_to_all | solution.py:13
  224.1 0.5 copy.154
  224.6 0.3 reshape.357
  224.9 1.5 fusion.49
  226.6 1.1 fusion.54
  227.7 1.9 collective-permute-start
  230.3 5.8 %collective-permute-done = bf16[256,2,128]{2,0,1:T(8,128)(2,1)S(1)} collective-permute-done((bf16[256,2,128]{2,0,1:T(8,128)(2,1)S(1)}, bf16[256,2,128]{2,0,1:T(8,128)(2,1)S(1)}, u32[]{:S(2)}, u32[]{:S(2)}) %collective-permute-start) | collective-permute-done | bytes 131104 | tf_op jit(solution)/shard_map/ppermute | solution.py:181
  236.1 0.8 bitcast_reduce_fusion
  236.9 1.4 fusion.1
  238.4 1.9 fusion.22
  240.5 0.7 copy.161
  241.2 1.2 copy.212
  (68 shorter events, 2.9 us)
Async XLA Ops:
  6.5 24.4 %copy-start = (s32[512,128]{1,0:T(8,128)S(1)}, s32[512,128]{1,0:T(8,128)}, u32[]{:S(2)}) copy-start(s32[512,128]{1,0:T(8,128)} %param.16) | copy-start | bytes 786436
  6.5 34.5 %copy-start.7 = (bf16[512,2,256]{2,1,0:T(2,128)(2,1)S(1)}, bf16[512,2,256]{2,1,0:T(2,128)(2,1)}, u32[]{:S(2)}) copy-start(bf16[512,2,256]{2,1,0:T(2,128)(2,1)} %param.27) | copy-start | bytes 1572868
  6.5 125.9 %all-gather.3.cloned.1.call-start = ((), (), s32[]{:S(2)}) async-start(), calls=%async_computation.5 | async-start | bytes 10526720 | tf_op jit(solution)/shard_map/all_gather | solution.py:114
  10.4 20.3 %all-to-all-start = ((s32[64,1,16]{2,1,0:T(1,128)}), s32[64,1,16]{2,1,0:T(1,128)S(1)}, u32[]{:S(2)}, u32[]{:S(2)}) async-start(s32[64,1,16]{2,1,0:T(1,128)} %broadcast_in_dim.81), calls=%async_computation | async-start | bytes 65536 | tf_op jit(solution)/shard_map/all_to_all | solution.py:13
  35.4 15.1 %all-to-all-start.1 = ((s32[64,1,384]{2,1,0:T(1,128)}), s32[64,1,384]{2,1,0:T(1,128)S(1)}, u32[]{:S(2)}, u32[]{:S(2)}) async-start(s32[64,1,384]{2,1,0:T(1,128)} %copy.136), calls=%async_computation.1 | async-start | bytes 196608 | tf_op jit(solution)/shard_map/all_to_all | solution.py:13
  50.6 19.2 %all-to-all-start.3 = ((bf16[4,128,512]{2,1,0:T(8,128)(2,1)}), bf16[4,128,512]{2,1,0:T(8,128)(2,1)S(1)}, u32[]{:S(2)}, u32[]{:S(2)}) async-start(bf16[4,128,512]{2,1,0:T(8,128)(2,1)} %reshape.350), calls=%async_computation.3 | async-start | bytes 1048576 | tf_op jit(solution)/shard_map/all_to_all | solution.py:13
  55.8 11.1 %copy-start.10 = (bf16[32,256]{1,0:T(8,128)(2,1)S(1)}, bf16[32,256]{1,0:T(8,128)(2,1)}, u32[]{:S(2)}) copy-start(bf16[32,256]{1,0:T(8,128)(2,1)} %param.22) | copy-start | bytes 49156
  67.0 7.6 %copy-start.9 = (f32[1024]{0:T(1024)S(1)}, f32[1024]{0:T(1024)}, u32[]{:S(2)}) copy-start(f32[1024]{0:T(1024)} %param.23) | copy-start | bytes 12292
  69.8 20.2 %all-to-all-start.2 = ((bf16[4,512,256]{2,1,0:T(8,128)(2,1)}), bf16[4,512,256]{2,1,0:T(8,128)(2,1)S(1)}, u32[]{:S(2)}, u32[]{:S(2)}) async-start(bf16[4,512,256]{2,1,0:T(8,128)(2,1)} %bitcast.7), calls=%async_computation.2 | async-start | bytes 2097152 | tf_op jit(solution)/shard_map/all_to_all | solution.py:13
  182.9 1.0 copy-start.8
  182.9 0.9 copy-start.11
  193.2 1.7 copy-start.6
  194.9 2.7 %copy-start.4 = (f32[4,128,1024]{2,1,0:T(8,128)S(1)}, f32[4,128,1024]{2,1,0:T(8,128)}, u32[]{:S(2)}) copy-start(f32[4,128,1024]{2,1,0:T(8,128)} %reshape.369) | copy-start | bytes 6291460
  202.9 5.7 %copy-start.5 = (bf16[512,1024]{1,0:T(8,128)(2,1)S(1)}, bf16[512,1024]{1,0:T(8,128)(2,1)}, u32[]{:S(2)}) copy-start(bf16[512,1024]{1,0:T(8,128)(2,1)} %param.28) | copy-start | bytes 3145732
  204.4 19.8 %all-to-all-start.4 = ((bf16[4,512,256]{1,2,0:T(8,128)(2,1)}), bf16[4,512,256]{1,2,0:T(8,128)(2,1)S(1)}, u32[]{:S(2)}, u32[]{:S(2)}) async-start(bf16[4,512,256]{1,2,0:T(8,128)(2,1)} %bitcast.37), calls=%async_computation.4 | async-start | bytes 2097152 | tf_op jit(solution)/shard_map/all_to_all | solution.py:13
  208.6 1.3 copy-start.12
  208.9 1.0 copy-start.3
  224.9 1.5 copy-start.2
  226.6 3.5 %slice-start = ((bf16[8,256,2,128]{3,2,1,0:T(2,128)(2,1)}), bf16[7,256,2,128]{3,2,1,0:T(2,128)(2,1)S(1)}, s32[]{:S(2)}) async-start(bf16[8,256,2,128]{3,2,1,0:T(2,128)(2,1)} %copy-done.2), calls=%async_computation.6 | async-start | bytes 1835008 | tf_op jit(solution)/shard_map/slice | solution.py:184
  227.7 8.4 %collective-permute-start = (bf16[256,2,128]{2,0,1:T(8,128)(2,1)S(1)}, bf16[256,2,128]{2,0,1:T(8,128)(2,1)S(1)}, u32[]{:S(2)}, u32[]{:S(2)}) collective-permute-start(bf16[256,2,128]{2,0,1:T(8,128)(2,1)S(1)} %bitcast.217), channel_id=1, source_target_pairs={{0,4},{4,8},{8,12},{12,16},{16,20},{20,24},{24,28},{28,32},{32,36}... | collective-permute-start | bytes 393224 | tf_op jit(solution)/shard_map/ppermute | solution.py:181
  240.3 2.1 copy-start.1
Sparse Core Ops, SparseCore 0:
  11.1 121.3 all-gather.2

commit v2 on v1

v2 whole, which is shorter than its diff:
```python
import functools
import math

import jax
import jax.numpy as jnp
from jax import lax
from jax.experimental import pallas as pl
from jax.experimental.pallas import tpu as pltpu
from jax.sharding import PartitionSpec as P

HD = 128
SHARE = 16
SCALE = 1.0 / math.sqrt(HD)


def exchange(value, axis):
    return lax.all_to_all(value, axis, split_axis=0, concat_axis=0, tiled=True)


def assemble(refs, place_ref, target, first, count):
    for r, ref in enumerate(refs):
        slots = ref.shape[0]

        def copy(slot, carry, ref=ref, r=r):
            row = pl.multiple_of(place_ref[r, slot] * SHARE, SHARE)
            for a in range(count):
                target[first + a, pl.ds(row, SHARE), :] = ref[slot, pl.ds(a * SHARE, SHARE), :]
            return carry

        lax.fori_loop(0, slots, copy, 0, unroll=8)


def encoder_body(
    parts, my_units, length, cond_len, place_ref, xs_ref, bias_ref, emb_ref, gain_ref, hit_ref, cond_ref, *refs
):
    wa_refs, wo_refs, wc_refs = refs[:parts], refs[parts : 2 * parts], refs[2 * parts : 3 * parts]
    out_ref, normed_ref, acc_ref, enc_ref, mixed_ref, buf_ref = refs[3 * parts :]
    step = pl.program_id(0)
    pieces, rows, columns = emb_ref.shape
    width = pieces * columns
    nt = (((1,), (1,)), ((), ()))
    nn = (((1,), (0,)), ((), ()))

    @pl.when(step == 0)
    def _():
        for n in range(my_units):
            here = pl.ds(n * length, length)
            value = jnp.concatenate(
                [emb_ref[t, here, :].astype(jnp.float32) for t in range(pieces)], axis=1
            )
            acc_ref[here, :] = value
            mean = jnp.sum(value * value, axis=1, keepdims=True) * (1.0 / width)
            normed_ref[here, :] = (value * lax.rsqrt(mean + 1e-05) * gain_ref[...]).astype(jnp.bfloat16)

    @pl.when(step < pieces)
    def _():
        head = xs_ref[step] * (columns // HD)
        assemble(wa_refs, place_ref, buf_ref, 0, 3)
        assemble(wo_refs, place_ref, buf_ref, 3, 1)
        normed = normed_ref[...]
        project = lambda a: lax.dot_general(
            normed, buf_ref[a], nn, preferred_element_type=jnp.float32
        ).astype(jnp.bfloat16)
        query, key, value = project(0), project(1), project(2)
        for h in range(columns // HD):
            cols = slice(h * HD, (h + 1) * HD)
            bias = bias_ref[head + h]
            for n in range(my_units):
                here = slice(n * length, (n + 1) * length)
                block = n * length // (rows // (cond_ref.shape[1] // cond_len))
                cond_rows = pl.ds(block * cond_len, cond_len)
                q = query[here, cols]
                self_scores = lax.dot_general(
                    q, key[here, cols], nt, preferred_element_type=jnp.float32
                ) * SCALE + bias * hit_ref[here, :].astype(jnp.float32)
                cond_scores = (
                    lax.dot_general(
                        q,
                        cond_ref[0, cond_rows, pl.ds(h * HD, HD)],
                        nt,
                        preferred_element_type=jnp.float32,
                    )
                    * SCALE
                )
                top = jnp.maximum(
                    jnp.max(self_scores, axis=1, keepdims=True),
                    jnp.max(cond_scores, axis=1, keepdims=True),
                )
                self_e = jnp.exp(self_scores - top)
                cond_e = jnp.exp(cond_scores - top)
                inverse = 1.0 / (
                    jnp.sum(self_e, axis=1, keepdims=True) + jnp.sum(cond_e, axis=1, keepdims=True)
                )
                mixed = lax.dot_general(
                    (self_e * inverse).astype(jnp.bfloat16),
                    value[here, cols],
                    nn,
                    preferred_element_type=jnp.float32,
                ) + lax.dot_general(
                    (cond_e * inverse).astype(jnp.bfloat16),
                    cond_ref[0, cond_rows, pl.ds(columns + h * HD, HD)],
                    nn,
                    preferred_element_type=jnp.float32,
                )
                mixed_ref[here, cols] = mixed.astype(jnp.bfloat16)
        acc_ref[...] += lax.dot_general(
            mixed_ref[...], buf_ref[3], nt, preferred_element_type=jnp.float32
        )

    @pl.when(step == pieces)
    def _():
        enc_ref[...] = acc_ref[...].astype(jnp.bfloat16)

    @pl.when(step >= pieces)
    def _():
        assemble(wc_refs, place_ref, buf_ref, 4, 1)
        out_ref[0] = lax.dot_general(
            enc_ref[...], buf_ref[4], nn, preferred_element_type=jnp.float32
        ).astype(jnp.bfloat16)


def encoder(place, xs, bias, emb, gain, hit, cond, weights, x_dim, my_units, length, cond_len):
    pieces, rows, columns = emb.shape
    width = pieces * columns
    last = pieces - 1
    full = lambda shape: pl.BlockSpec(shape, lambda i, p, x: (0,) * len(shape))
    specs = {"a": [], "o": [], "c": []}
    arrays = {"a": [], "o": [], "c": []}
    for kind, array, height, index in weights:
        slots = array.shape[1 - x_dim]
        pick = (
            (lambda i: jnp.minimum(i, last)) if kind in "ao" else (lambda i: jnp.maximum(i - pieces, 0))
        )
        if x_dim == 0:
            shape = (None, slots, height, columns)
            mapping = lambda i, p, x, pick=pick, index=index: (pick(i), 0, index, 0)
        else:
            shape = (slots, None, height, columns)
            mapping = lambda i, p, x, pick=pick, index=index: (0, pick(i), index, 0)
        specs[kind].append(pl.BlockSpec(shape, mapping))
        arrays[kind].append(array)
    parts = len(specs["a"])
    return pl.pallas_call(
        functools.partial(encoder_body, parts, my_units, length, cond_len),
        out_shape=jax.ShapeDtypeStruct((pieces, rows, columns), jnp.bfloat16),
        grid_spec=pltpu.PrefetchScalarGridSpec(
            num_scalar_prefetch=2,
            grid=(2 * pieces,),
            in_specs=[
                pl.BlockSpec(memory_space=pltpu.SMEM),
                full(emb.shape),
                full(gain.shape),
                full(hit.shape),
                pl.BlockSpec(
                    (1,) + cond.shape[1:], lambda i, p, x: (x[jnp.minimum(i, last)], 0, 0)
                ),
                *specs["a"],
                *specs["o"],
                *specs["c"],
            ],
            out_specs=pl.BlockSpec(
                (1, rows, columns), lambda i, p, x: (x[jnp.maximum(i - pieces, 0)], 0, 0)
            ),
            scratch_shapes=[
                pltpu.VMEM((rows, width), jnp.bfloat16),
                pltpu.VMEM((rows, width), jnp.float32),
                pltpu.VMEM((rows, width), jnp.bfloat16),
                pltpu.VMEM((rows, columns), jnp.bfloat16),
                pltpu.VMEM((5, width, columns), jnp.bfloat16),
            ],
        ),
        compiler_params=pltpu.CompilerParams(
            dimension_semantics=("arbitrary",), vmem_limit_bytes=48 * 1024 * 1024
        ),
        name="encoder",
    )(place, xs, bias, emb, gain, hit, cond, *arrays["a"], *arrays["o"], *arrays["c"])


def attend_body(heads, allowed_ref, q_ref, cur_ref, prev_ref, carried_ref, out_ref):
    block = pl.program_id(0)
    nt = (((1,), (1,)), ((), ()))
    nn = (((1,), (0,)), ((), ()))
    tokens = q_ref.shape[0]
    previous = jnp.where(block == 0, carried_ref[...], prev_ref[...])

    def mix(query, kv):
        scores = (
            lax.dot_general(query, kv[:, :HD], nt, preferred_element_type=jnp.float32) * SCALE
        )
        e = jnp.exp(scores - jnp.max(scores, axis=1, keepdims=True))
        weights = (e * (1.0 / jnp.sum(e, axis=1, keepdims=True))).astype(jnp.bfloat16)
        return lax.dot_general(weights, kv[:, HD:], nn, preferred_element_type=jnp.float32)

    query = jnp.concatenate([q_ref[:, pl.ds(h * HD, HD)] for h in range(heads)], axis=0)
    leading = mix(query, previous)
    leading = jnp.where(allowed_ref[block] > 0, leading, jnp.zeros_like(leading))
    final = jnp.concatenate(
        [q_ref[tokens - 8 :, pl.ds(h * HD, HD)].astype(jnp.float32)[7:8] for h in range(heads)], axis=0
    ).astype(jnp.bfloat16)
    trailing = mix(final, cur_ref[...])
    row = lax.broadcasted_iota(jnp.int32, (tokens, HD), 0)
    for h in range(heads):
        out_ref[:, pl.ds(h * HD, HD)] = jnp.where(
            row == tokens - 1,
            jnp.broadcast_to(trailing[h : h + 1], (tokens, HD)),
            leading[h * tokens : (h + 1) * tokens],
        ).astype(jnp.bfloat16)


def attend(allowed, queries, keys_values, carried, key_rows):
    block_count = allowed.shape[0]
    tokens = queries.shape[0] // block_count
    heads = queries.shape[1] // HD
    return pl.pallas_call(
        functools.partial(attend_body, heads),
        out_shape=jax.ShapeDtypeStruct(queries.shape, jnp.bfloat16),
        grid=(block_count,),
        in_specs=[
            pl.BlockSpec(memory_space=pltpu.SMEM),
            pl.BlockSpec((tokens, queries.shape[1]), lambda c: (c, 0)),
            pl.BlockSpec((key_rows, 2 * HD), lambda c: (c, 0)),
            pl.BlockSpec((key_rows, 2 * HD), lambda c: (jnp.maximum(c - 1, 0), 0)),
            pl.BlockSpec((key_rows, 2 * HD), lambda c: (0, 0)),
        ],
        out_specs=pl.BlockSpec((tokens, queries.shape[1]), lambda c: (c, 0)),
        compiler_params=pltpu.CompilerParams(dimension_semantics=("arbitrary",)),
        name="attend",
    )(allowed, queries, keys_values, keys_values, carried)


def shards(
    db_tokens,
    db_parent,
    db_depth,
    nb_rows,
    seq_start,
    table,
    depth_table,
    enc_gain,
    enc_qkv,
    tree_bias,
    enc_wo,
    cond_kv,
    queries,
    cca_kv,
):
    seq_size = lax.axis_size("seq")
    tp_size = lax.axis_size("tp")
    block_count, pair_count = nb_rows.shape
    unit_count = block_count * pair_count
    stored, length = db_tokens.shape
    columns = table.shape[1]
    width = columns * tp_size
    rows_here = enc_qkv.shape[0]

    share = jnp.concatenate(
        [
            enc_qkv.transpose(1, 0, 2).reshape(3 * rows_here, columns),
            enc_wo.T,
            cca_kv.reshape(rows_here, columns),
        ],
        axis=0,
    )
    shares = lax.all_gather(share, ("seq", "tp"), axis=0).reshape(
        seq_size, tp_size, 5 * rows_here, columns
    )
    kv_cols = cca_kv.shape[2]

    cond_len = cond_kv.shape[0] // block_count
    my_blocks = block_count // tp_size
    cond = exchange(
        cond_kv.reshape(tp_size, my_blocks * cond_len, 2 * columns), "tp"
    )

    flat_rows = nb_rows.reshape(unit_count)
    holder = flat_rows // stored
    local_row = flat_rows % stored
    places = jnp.arange(seq_size, dtype=jnp.int32)
    request = jnp.sum(
        jnp.where(holder[None, :] == places[:, None], local_row[None, :], 0), axis=1
    )
    request = jnp.broadcast_to(request[:, None], (seq_size, 16))
    wanted = exchange(request, "seq")[:, 0]
    reply = jnp.concatenate(
        [
            jnp.take(db_tokens, wanted, axis=0),
            jnp.take(db_depth, wanted, axis=0),
            jnp.take(db_parent, wanted, axis=0),
        ],
        axis=1,
    )
    fetched = jnp.take(exchange(reply, "seq"), holder, axis=0)
    tokens = fetched[:, :length].reshape(unit_count * length)
    depths = fetched[:, length : 2 * length].reshape(unit_count * length)
    parents = fetched[:, 2 * length :]
    depth_hit = (
        depths[:, None] == jnp.arange(depth_table.shape[0], dtype=jnp.int32)[None, :]
    ).astype(jnp.bfloat16)
    embedded = (
        jnp.take(table, tokens, axis=0).astype(jnp.float32)
        + jnp.dot(depth_hit, depth_table, preferred_element_type=jnp.float32)
    ).astype(jnp.bfloat16)

    my_units = unit_count // tp_size
    pieces = exchange(embedded.reshape(tp_size, my_units * length, columns), "tp")
    parents = lax.dynamic_slice_in_dim(parents, lax.axis_index("tp") * my_units, my_units)
    parent_hit = (
        parents.reshape(my_units * length)[:, None] == jnp.arange(length, dtype=parents.dtype)[None, :]
    ).astype(jnp.bfloat16)
    place = jnp.arange(seq_size, dtype=jnp.int32)[None]
    outgoing = encoder(
        place,
        jnp.arange(tp_size, dtype=jnp.int32),
        tree_bias,
        pieces,
        enc_gain[None],
        parent_hit,
        cond,
        [("a", shares, 3 * SHARE, 0), ("o", shares, SHARE, 3), ("c", shares, SHARE, 4)],
        1,
        my_units,
        length,
        cond_len,
    )
    key_rows = pair_count * length
    keys_values = exchange(outgoing, "tp").reshape(unit_count * length, 2 * kv_cols)
    carried = lax.ppermute(
        keys_values[(block_count - 1) * key_rows :], "seq", [(s, s + 1) for s in range(seq_size - 1)]
    )
    block_index = lax.axis_index("seq") * block_count + jnp.arange(block_count, dtype=jnp.int32)
    allowed = (block_index > 0) & (seq_start == 0)
    return attend(allowed.astype(jnp.int32), queries, keys_values, carried, key_rows)


def solution(mesh):
    in_specs = (
        P("seq", None),
        P("seq", None),
        P("seq", None),
        P("seq", None),
        P("seq"),
        P(None, "tp"),
        P(None, "tp"),
        P(),
        P("seq", None, "tp"),
        P(),
        P("tp", "seq"),
        P("seq", None, "tp"),
        P("seq", "tp"),
        P("seq", None, "tp"),
    )
    out_specs = P("seq", "tp")
    return jax.shard_map(shards, mesh=mesh, in_specs=in_specs, out_specs=out_specs, check_vma=False)
```

time: 250 us -> 204 us (0.82)
  local copies, waits for them, and re-layouts: 84.7 us -> 21.5 us
  Pallas kernels: 0 us -> 34.7 us
  matrix products: 23.9 us -> 2.8 us
  waiting for transfers between devices: 86.7 us -> 95 us
  other arithmetic: 7.25 us -> 2.42 us
    pallas_call x0 -> x2, Pallas kernels: none -> 34.7 us  [the longest x1 26.2 us: encoder(): pl.pallas_call(functools.partial(encoder_body, parts, my_units, length, c...]
    transpose x5 -> x0, local copies, waits for them, and re-layouts: 27 us -> none  [the longest x2 18 us: shards(): w_qkv = shares[:, :, :3].transpose(0, 3, 2, 1, 4).reshape(width, 3, width)]
    dot_general x10 -> x0, matrix products: 21.1 us -> none  [the longest x1 6.4 us: encoder_mix(): jnp.einsum('une,eaf->unaf', normed, w_qkv, preferred_element_type=jnp.flo...]
    reshape x7 -> x0, local copies, waits for them, and re-layouts: 18.6 us -> none  [the longest x1 11 us: shards(): w_qkv = shares[:, :, :3].transpose(0, 3, 2, 1, 4).reshape(width, 3, width)]
    all_gather x1, waiting for transfers between devices: 36.6 us -> 42.5 us  [shards(): lax.all_gather(share, ('seq', 'tp'), axis=0)]
    another operation x2 -> x0, local copies, waits for them, and re-layouts: 5 us -> none  [shards(): w_cca = shares[:, :, 4].reshape(seq_size, tp_size, rows_here, 2, kv_cols)...]
    convert_element_type x4 -> x0, local copies, waits for them, and re-layouts: 4.31 us -> none  [the longest x2 3.48 us: shards(): encoded = (embedded.astype(jnp.float32) + increment).astype(jnp.bfloat16)]
    unnamed x35 -> x17, local copies, waits for them, and re-layouts: 6.31 us -> 2.2 us
where the time goes in v2:
time: 204 us; the launch traced here: 203 us
  waiting for transfers between devices  95 us (47%)
  Pallas kernels  34.7 us (17%)
  starting transfers between devices  32.8 us (16%)
  local copies, waits for them, and re-layouts  21.5 us (11%)
  between operations  13.6 us (7%)
  matrix products  2.8 us (1%)
  other arithmetic  2.42 us (1%)
    all_to_all x5, waiting for transfers between devices, exchange(): return lax.all_to_all(value, axis, split_axis=0, concat_axis=0, tiled=True)  46.6 us
    all_gather x1, waiting for transfers between devices, shards(): lax.all_gather(share, ('seq', 'tp'), axis=0)  42.5 us
    all_to_all x5, starting transfers between devices, exchange(): return lax.all_to_all(value, axis, split_axis=0, concat_axis=0, tiled=True)  30.9 us
    pallas_call x1, Pallas kernels, encoder(): pl.pallas_call(functools.partial(encoder_body, parts, my_units, length, c...  26.2 us
    gather x1, local copies, waits for them, and re-layouts, shards(): jnp.take(table, tokens, axis=0).astype(jnp.float32)  11.1 us
    pallas_call x1, Pallas kernels, attend(): pl.pallas_call(functools.partial(attend_body, heads), out_shape=jax.Shape...  8.52 us
    ppermute x1, waiting for transfers between devices, shards(): lax.ppermute(keys_values[(block_count - 1) * key_rows:], 'seq', [(s, s +...  5.88 us
  transfers between devices with their start and end apart: 7, of which 6 were waited for; matrix products, arithmetic and copies ran while one was open for 12% of the time, Pallas kernels for 0%

profile of v2, /device:TPU:32, one launch (start us, length us, event | category | flops | bytes accessed | tf_op | source)
XLA Modules:
  0.0 202.9 jit_solution(11942561932075954016)
XLA Ops:
  6.5 0.0 copy-start
  6.5 0.0 copy-start.5
  6.5 0.0 all-gather.3.cloned.1.call-start
  6.5 0.7 copy.33
  7.3 1.4 pad_maximum_fusion
  8.6 0.0 all-gather.3.cloned.1.call-update
  8.7 0.8 copy.25
  9.4 0.1 reshape.211
  9.5 0.1 select_reduce_fusion
  9.6 0.8 broadcast_in_dim.59
  10.4 11.8 %all-to-all-start = ((s32[64,1,16]{2,1,0:T(1,128)}), s32[64,1,16]{2,1,0:T(1,128)S(1)}, u32[]{:S(2)}, u32[]{:S(2)}) async-start(s32[64,1,16]{2,1,0:T(1,128)} %broadcast_in_dim.59), calls=%async_computation | async-start | bytes 65536 | tf_op jit(solution)/shard_map/all_to_all | solution.py:17
  22.2 0.1 reshape.212
  22.2 8.5 %all-to-all-done = s32[64,1,16]{2,1,0:T(1,128)S(1)} async-done(((s32[64,1,16]{2,1,0:T(1,128)}), s32[64,1,16]{2,1,0:T(1,128)S(1)}, u32[]{:S(2)}, u32[]{:S(2)}) %all-to-all-start) | async-done | bytes 4128 | tf_op jit(solution)/shard_map/all_to_all | solution.py:17
  30.7 0.1 slice_reduce_fusion
  30.9 0.0 copy-done
  30.9 0.6 gather_fusion.2
  31.5 1.5 gather_fusion.3
  33.0 1.5 gather_fusion.4
  34.6 0.1 broadcast_select_fusion.2
  34.7 0.7 copy.26
  35.4 5.5 %all-to-all-start.1 = ((s32[64,1,384]{2,1,0:T(1,128)}), s32[64,1,384]{2,1,0:T(1,128)S(1)}, u32[]{:S(2)}, u32[]{:S(2)}) async-start(s32[64,1,384]{2,1,0:T(1,128)} %copy.26), calls=%async_computation.1 | async-start | bytes 196608 | tf_op jit(solution)/shard_map/all_to_all | solution.py:17
  41.0 0.0 copy-start.1
  41.0 0.0 copy-start.2
  41.0 2.2 %reshape.216 = bf16[4,128,512]{2,1,0:T(8,128)(2,1)} reshape(bf16[512,2,256]{2,1,0:T(2,128)(2,1)} %param.27) | data formatting | bytes 1048576 | tf_op jit(solution)/shard_map/reshape | solution.py:272
  43.2 7.4 %all-to-all-done.1 = s32[64,1,384]{2,1,0:T(1,128)S(1)} async-done(((s32[64,1,384]{2,1,0:T(1,128)}), s32[64,1,384]{2,1,0:T(1,128)S(1)}, u32[]{:S(2)}, u32[]{:S(2)}) %all-to-all-start.1) | async-done | bytes 98336 | tf_op jit(solution)/shard_map/all_to_all | solution.py:17
  50.5 4.5 %all-to-all-start.3 = ((bf16[4,128,512]{2,1,0:T(8,128)(2,1)}), bf16[4,128,512]{2,1,0:T(8,128)(2,1)S(1)}, u32[]{:S(2)}, u32[]{:S(2)}) async-start(bf16[4,128,512]{2,1,0:T(8,128)(2,1)} %reshape.216), calls=%async_computation.3 | async-start | bytes 1048576 | tf_op jit(solution)/shard_map/all_to_all | solution.py:17
  55.1 0.6 gather_fusion
  55.7 0.1 broadcast_select_fusion.3
  55.8 11.1 %gather_fusion.1 = bf16[2048,256]{1,0:T(8,128)(2,1)S(1)} fusion(bf16[16384,256]{1,0:T(8,128)(2,1)} %param.21, s32[2048]{0:T(1024)S(1)} %broadcast_clamp_fusion), kind=kCustom, calls=%fused_computation.4 | custom fusion | bytes 2105344 | tf_op jit(solution)/shard_map/jit(_take)/gather | solution.py:300
  66.9 0.0 copy-done.5
  66.9 2.8 %fusion = bf16[2048,256]{1,0:T(8,128)(2,1)} fusion(bf16[32,256]{1,0:T(8,128)(2,1)S(1)} %copy-done.5, bf16[2048,256]{1,0:T(8,128)(2,1)S(1)} %gather_fusion.1, pred[2048]{0:T(1024)(128)(4,1)S(1)} %compare_and_fusion, s32[2048]{0:T(1024)S(1)} %get-tuple-element.9), kind=kOutput, calls=%fused_computation.6 | convolution fusion | flops 35717120 | bytes 2123776 | tf_op jit(solution)/shard_map/dot_general | solution.py:301
  69.7 0.0 all-to-all-done.3.cond_ref
  69.7 4.8 %all-to-all-start.2 = ((bf16[4,512,256]{2,1,0:T(8,128)(2,1)}), bf16[4,512,256]{2,1,0:T(8,128)(2,1)S(1)}, u32[]{:S(2)}, u32[]{:S(2)}) async-start(bf16[4,512,256]{2,1,0:T(8,128)(2,1)} %bitcast.7), calls=%async_computation.2 | async-start | bytes 2097152 | tf_op jit(solution)/shard_map/all_to_all | solution.py:17
  74.5 0.1 fusion.2.hit_ref
  74.6 15.2 %all-to-all-done.2.emb_ref = bf16[4,512,256]{2,1,0:T(8,128)(2,1)S(1)} async-done(((bf16[4,512,256]{2,1,0:T(8,128)(2,1)}), bf16[4,512,256]{2,1,0:T(8,128)(2,1)S(1)}, u32[]{:S(2)}, u32[]{:S(2)}) %all-to-all-start.2) | async-done | bytes 1048608 | tf_op jit(solution)/shard_map/all_to_all | solution.py:17
  89.9 42.5 %all-gather.3.cloned.1.call-done = bf16[20480,256]{1,0:T(8,128)(2,1)} async-done(((bf16[80,256]{1,0:T(8,128)(2,1)}), bf16[20480,256]{1,0:T(8,128)(2,1)}) %all-gather.3.cloned.1.call-update) | async-done | bytes 10485776 | tf_op jit(solution)/shard_map/all_gather | solution.py:264
  132.4 0.0 copy-done.1
  132.4 0.0 copy-done.2
  132.4 0.0 copy-start.6
  132.4 26.2 %encoder.1 = bf16[4,512,256]{2,1,0:T(8,128)(2,1)} custom-call(s32[1,64]{1,0:T(1,128)S(1)} %iota.23.place_ref, s32[4]{0:T(128)S(1)} %iota.24.xs_ref, f32[8]{0:T(128)S(1)} %copy-done.2, bf16[4,512,256]{2,1,0:T(8,128)(2,1)S(1)} %all-to-all-done.2.emb_ref, f32[1,1024]{1,0:T(1,128)S(1)} %bitcast.31, bf16[512,128]{1,0:T(8,128)(2,1)S(1)} %fusion.2.hit_ref, ...), custom_call_target="tpu_custom_call" | custom-call | tf_op jit(solution)/shard_map/encoder/pallas_call | solution.py:143
  158.6 4.3 %all-to-all-start.4 = ((bf16[4,512,256]{2,1,0:T(8,128)(2,1)}), bf16[4,512,256]{2,1,0:T(8,128)(2,1)S(1)}, u32[]{:S(2)}, u32[]{:S(2)}) async-start(bf16[4,512,256]{2,1,0:T(8,128)(2,1)} %encoder.1), calls=%async_computation.4 | async-start | bytes 2097152 | tf_op jit(solution)/shard_map/all_to_all | solution.py:17
  162.9 15.5 %all-to-all-done.4 = bf16[4,512,256]{2,1,0:T(8,128)(2,1)S(1)} async-done(((bf16[4,512,256]{2,1,0:T(8,128)(2,1)}), bf16[4,512,256]{2,1,0:T(8,128)(2,1)S(1)}, u32[]{:S(2)}, u32[]{:S(2)}) %all-to-all-start.4) | async-done | bytes 1048608 | tf_op jit(solution)/shard_map/all_to_all | solution.py:17
  178.4 0.0 copy-start.3
  178.4 1.9 collective-permute-start
  180.4 0.0 copy-done.6
  180.4 0.6 and_convert_fusion.allowed_ref
  180.9 5.9 %collective-permute-done.carried_ref = bf16[256,256]{1,0:T(8,128)(2,1)S(1)} collective-permute-done((bf16[256,256]{1,0:T(8,128)(2,1)S(1)}, bf16[256,256]{1,0:T(8,128)(2,1)S(1)}, u32[]{:S(2)}, u32[]{:S(2)}) %collective-permute-start) | collective-permute-done | bytes 131104 | tf_op jit(solution)/shard_map/ppermute | solution.py:327
  186.8 0.0 copy-done.3
  186.8 0.0 copy-start.4
  186.8 0.7 copy-done.4
  187.5 8.5 %attend.1 = bf16[512,1024]{1,0:T(8,128)(2,1)} custom-call(s32[8]{0:T(128)} %and_convert_fusion.allowed_ref, bf16[512,1024]{1,0:T(8,128)(2,1)} %q_ref.1, bf16[2048,256]{1,0:T(8,128)(2,1)} %bitcast.36, bf16[2048,256]{1,0:T(8,128)(2,1)} %bitcast.37, bf16[256,256]{1,0:T(8,128)(2,1)} %copy-done.4), custom_call_target="tpu_custom_call" | custom-call | tf_op jit(solution)/shard_map/attend/pallas_call | solution.py:214
  (17 shorter events, 0.1 us)
Async XLA Ops:
  6.5 24.3 %copy-start = (s32[512,128]{1,0:T(8,128)S(1)}, s32[512,128]{1,0:T(8,128)}, u32[]{:S(2)}) copy-start(s32[512,128]{1,0:T(8,128)} %param.16) | copy-start | bytes 786436
  6.5 60.4 %copy-start.5 = (bf16[32,256]{1,0:T(8,128)(2,1)S(1)}, bf16[32,256]{1,0:T(8,128)(2,1)}, u32[]{:S(2)}) copy-start(bf16[32,256]{1,0:T(8,128)(2,1)} %param.22) | copy-start | bytes 49156
  6.5 125.9 %all-gather.3.cloned.1.call-start = ((), (), s32[]{:S(2)}) async-start(), calls=%async_computation.5 | async-start | bytes 10526720 | tf_op jit(solution)/shard_map/all_gather | solution.py:264
  10.4 20.3 %all-to-all-start = ((s32[64,1,16]{2,1,0:T(1,128)}), s32[64,1,16]{2,1,0:T(1,128)S(1)}, u32[]{:S(2)}, u32[]{:S(2)}) async-start(s32[64,1,16]{2,1,0:T(1,128)} %broadcast_in_dim.59), calls=%async_computation | async-start | bytes 65536 | tf_op jit(solution)/shard_map/all_to_all | solution.py:17
  35.4 15.1 %all-to-all-start.1 = ((s32[64,1,384]{2,1,0:T(1,128)}), s32[64,1,384]{2,1,0:T(1,128)S(1)}, u32[]{:S(2)}, u32[]{:S(2)}) async-start(s32[64,1,384]{2,1,0:T(1,128)} %copy.26), calls=%async_computation.1 | async-start | bytes 196608 | tf_op jit(solution)/shard_map/all_to_all | solution.py:17
  41.0 91.5 %copy-start.1 = (f32[1024]{0:T(1024)S(1)}, f32[1024]{0:T(1024)}, u32[]{:S(2)}) copy-start(f32[1024]{0:T(1024)} %param.23) | copy-start | bytes 12292
  41.0 91.4 %copy-start.2 = (f32[8]{0:T(128)S(1)}, f32[8]{0:T(128)}, u32[]{:S(2)}) copy-start(f32[8]{0:T(128)} %bias_ref.1) | copy-start | bytes 100
  50.5 19.2 %all-to-all-start.3 = ((bf16[4,128,512]{2,1,0:T(8,128)(2,1)}), bf16[4,128,512]{2,1,0:T(8,128)(2,1)S(1)}, u32[]{:S(2)}, u32[]{:S(2)}) async-start(bf16[4,128,512]{2,1,0:T(8,128)(2,1)} %reshape.216), calls=%async_computation.3 | async-start | bytes 1048576 | tf_op jit(solution)/shard_map/all_to_all | solution.py:17
  69.7 20.2 %all-to-all-start.2 = ((bf16[4,512,256]{2,1,0:T(8,128)(2,1)}), bf16[4,512,256]{2,1,0:T(8,128)(2,1)S(1)}, u32[]{:S(2)}, u32[]{:S(2)}) async-start(bf16[4,512,256]{2,1,0:T(8,128)(2,1)} %bitcast.7), calls=%async_computation.2 | async-start | bytes 2097152 | tf_op jit(solution)/shard_map/all_to_all | solution.py:17
  132.4 47.9 %copy-start.6 = (s32[8]{0:T(128)S(1)}, s32[8]{0:T(128)}, u32[]{:S(2)}) copy-start(s32[8]{0:T(128)} %param.20) | copy-start | bytes 100
  158.6 19.8 %all-to-all-start.4 = ((bf16[4,512,256]{2,1,0:T(8,128)(2,1)}), bf16[4,512,256]{2,1,0:T(8,128)(2,1)S(1)}, u32[]{:S(2)}, u32[]{:S(2)}) async-start(bf16[4,512,256]{2,1,0:T(8,128)(2,1)} %encoder.1), calls=%async_computation.4 | async-start | bytes 2097152 | tf_op jit(solution)/shard_map/all_to_all | solution.py:17
  178.4 8.4 %copy-start.3 = (bf16[4,512,256]{2,1,0:T(8,128)(2,1)}, bf16[4,512,256]{2,1,0:T(8,128)(2,1)S(1)}, u32[]{:S(2)}) copy-start(bf16[4,512,256]{2,1,0:T(8,128)(2,1)S(1)} %all-to-all-done.4) | copy-start | bytes 3145732
  178.4 8.4 %collective-permute-start = (bf16[256,256]{1,0:T(8,128)(2,1)S(1)}, bf16[256,256]{1,0:T(8,128)(2,1)S(1)}, u32[]{:S(2)}, u32[]{:S(2)}) collective-permute-start(bf16[256,256]{1,0:T(8,128)(2,1)S(1)} %slice.34), channel_id=1, source_target_pairs={{0,4},{4,8},{8,12},{12,16},{16,20},{20,24},{24,28},{28,32},{32,36}... | collective-permute-start | bytes 393224 | tf_op jit(solution)/shard_map/ppermute | solution.py:327
  186.8 0.7 copy-start.4
Sparse Core Ops, SparseCore 0:
  11.1 121.3 all-gather.2
